TPU v7x, 32 devices: a whole 2x2x4 slice. The times are simulated.
32 devices in a mesh: tiles: 2 (over y), row: 8 (over z, x), col: 2 (over core).
Axes of the slice: x: 2, y: 2, z: 4, core: 2. Of those that a mesh axis runs over, the one named last changes fastest.
Arguments:
- layers: float32 [8, 4096, 4096], P('tiles', 'row', 'col'), parts along dimension 0, may hold values from -6 to 6
- unmixing: bfloat16 [4, 4, 4, 2048, 4096], P('tiles', None, None, ('row', 'col')), parts along dimension 0, may hold values from -2 to 2
Outputs:
- components: float32 [8, 4096, 4096], P('tiles', 'row', 'col'), parts along dimension 0
There are 2 independent parts, one for each index of `tiles`. A program takes and returns all parts, laid end to end along the dimension named above; each array names one. Nothing has to cross between parts.
All inputs are finite; a program needn't handle non-finite values.
Results may differ from a plain program's by a relative error of at most 0.0003.
Values sent between devices are 32-bit elements; how exact they have to be, the bound alone decides.
No kernel may reach another device: no remote copies, remote signals or barrier semaphores. Data moves between devices by JAX's collectives and lax.ppermute only.
A program may use at most 320 MiB of HBM per device.

v0:
```python
import math
import jax
import jax.numpy as jnp
from jax import lax
from jax.sharding import PartitionSpec as P


def phase_pair(first_len, second_len, period, sign):
    first = lax.broadcasted_iota(jnp.int32, (first_len, second_len), 0)
    second = lax.broadcasted_iota(jnp.int32, (first_len, second_len), 1)
    turns = (first * second % period).astype(jnp.float32)
    phase = turns * (sign * 2.0 * math.pi / period)
    return (jnp.cos(phase), jnp.sin(phase))


def contract_first(values, table):
    return jnp.einsum("...qp,qk->...pk", values, table, precision=lax.Precision.HIGHEST)


def contract_second(values, table):
    return jnp.einsum("...pk,pj->...jk", values, table, precision=lax.Precision.HIGHEST)


def fourier(real_in, imag_in, length, sign, in_len, out_len, real_only):
    inner_len = min(length, 128)
    outer_len = length // inner_len
    rows_in = in_len // outer_len
    rows_out = out_len // inner_len
    leading = real_in.shape[:-1]
    first_cos, first_sin = phase_pair(rows_in, inner_len, inner_len, sign)
    first_table = jnp.concatenate([first_cos, first_sin], axis=1)
    both = contract_first(real_in.reshape(leading + (rows_in, outer_len)), first_table)
    part_real = both[..., :inner_len]
    part_imag = both[..., inner_len:]
    if imag_in is not None:
        other = contract_first(imag_in.reshape(leading + (rows_in, outer_len)), first_table)
        part_real = part_real - other[..., inner_len:]
        part_imag = part_imag + other[..., :inner_len]
    twist_cos, twist_sin = phase_pair(outer_len, inner_len, length, sign)
    turned_real = part_real * twist_cos - part_imag * twist_sin
    turned_imag = part_real * twist_sin + part_imag * twist_cos
    stacked = jnp.concatenate([turned_real, turned_imag], axis=-2)
    second_cos, second_sin = phase_pair(outer_len, rows_out, outer_len, sign)
    table_real = jnp.concatenate([second_cos, -second_sin], axis=0)
    if real_only:
        result_real = contract_second(stacked, table_real)
        return result_real.reshape(leading + (out_len,))
    table_imag = jnp.concatenate([second_sin, second_cos], axis=0)
    combined = contract_second(stacked, jnp.concatenate([table_real, table_imag], axis=1))
    result_real = combined[..., :rows_out, :].reshape(leading + (out_len,))
    result_imag = combined[..., rows_out:, :].reshape(leading + (out_len,))
    return (result_real, result_imag)


def reorder_blocks(values, row_count, col_count):
    leading = values.shape[0]
    block = values.shape[1] // (row_count * col_count)
    width = values.shape[2]
    split = values.reshape(leading, col_count, row_count, block, width)
    return jnp.transpose(split, (0, 4, 2, 1, 3)).reshape(
        leading, width, row_count * col_count * block
    )


def shards(layers, unmixing):
    row_count = lax.axis_size("row")
    col_count = lax.axis_size("col")
    rows_len = layers.shape[1] * row_count
    cols_len = layers.shape[2] * col_count
    spec_real, spec_imag = fourier(
        lax.all_to_all(layers, "col", split_axis=1, concat_axis=2, tiled=True),
        None,
        cols_len,
        -1.0,
        cols_len,
        cols_len // 2,
        False,
    )
    moved_real, moved_imag = (
        lax.all_to_all(
            lax.all_to_all(spec_real, "row", split_axis=2, concat_axis=1, tiled=True),
            "col",
            split_axis=2,
            concat_axis=1,
            tiled=True,
        ),
        lax.all_to_all(
            lax.all_to_all(spec_imag, "row", split_axis=2, concat_axis=1, tiled=True),
            "col",
            split_axis=2,
            concat_axis=1,
            tiled=True,
        ),
    )
    line_real = reorder_blocks(moved_real, row_count, col_count)
    line_imag = reorder_blocks(moved_imag, row_count, col_count)
    wave_real, wave_imag = fourier(line_real, line_imag, rows_len, -1.0, rows_len, rows_len, False)
    mixed_real = None
    mixed_imag = None
    for layer_index in range(4):
        weight_real = unmixing[0, :, layer_index].astype(jnp.float32)
        weight_imag = unmixing[1, :, layer_index].astype(jnp.float32)
        layer_real = wave_real[layer_index][None]
        layer_imag = wave_imag[layer_index][None]
        term_real = weight_real * layer_real - weight_imag * layer_imag
        term_imag = weight_real * layer_imag + weight_imag * layer_real
        if mixed_real is None:
            mixed_real = term_real
            mixed_imag = term_imag
        else:
            mixed_real = mixed_real + term_real
            mixed_imag = mixed_imag + term_imag
    back_real, back_imag = fourier(mixed_real, mixed_imag, rows_len, 1.0, rows_len, rows_len, False)
    scale = 2.0 / (rows_len * cols_len)
    sent_real, sent_imag = (
        lax.all_to_all(
            lax.all_to_all(back_real, "row", split_axis=2, concat_axis=1, tiled=True),
            "col",
            split_axis=2,
            concat_axis=1,
            tiled=True,
        ),
        lax.all_to_all(
            lax.all_to_all(back_imag, "row", split_axis=2, concat_axis=1, tiled=True),
            "col",
            split_axis=2,
            concat_axis=1,
            tiled=True,
        ),
    )
    grid_real = reorder_blocks(sent_real, row_count, col_count)
    grid_imag = reorder_blocks(sent_imag, row_count, col_count)
    fields = fourier(grid_real, grid_imag, cols_len, 1.0, cols_len // 2, cols_len, True)
    fields = fields * scale
    return lax.all_to_all(fields, "col", split_axis=2, concat_axis=1, tiled=True)


def solution(mesh):
    in_specs = (P("tiles", "row", "col"), P("tiles", None, None, ("row", "col"), None))
    out_specs = P("tiles", "row", "col")
    return jax.shard_map(shards, mesh=mesh, in_specs=in_specs, out_specs=out_specs, check_vma=False)
```

profile of v0, /device:TPU:0, one launch (start us, length us, event | category | flops | bytes accessed | tf_op | source)
XLA Modules:
  0.0 1691.4 jit_solution(6777798758830967953)
XLA Ops:
  0.0 20.9 %copy.174 = f32[4,512,2048]{2,0,1:T(4,128)} copy(f32[4,512,2048]{2,1,0:T(8,128)} %param.2) | data formatting | bytes 33554432 | tf_op args[0]
  44.1 17.8 %copy.175 = f32[4,512,2048]{2,1,0:T(8,128)} copy(f32[4,512,2048]{2,0,1:T(4,128)} %all-to-all-done) | data formatting | bytes 33554432 | tf_op jit(solution)/shard_map/all_to_all | solution.py:71
  61.9 16.4 copy.176
  78.3 44.1 %fusion.8 = f32[4,256,32,256]{1,3,2,0:T(8,128)} fusion(f32[4,256,128,32]{1,3,2,0:T(8,128)} %bitcast.134, f32[128,128]{0,1:T(8,128)S(1)} %get-tuple-element.35, f32[128,128]{0,1:T(8,128)S(1)} %get-tuple-element.36), kind=kOutput, calls=%fused_computation.19 | convolution fusion | flops 12884934656 | bytes 50462720 | tf_op jit(solution)/shard_map/...qp,qk->...pk/dot_general | solution.py:17
  122.4 17.6 %multiply_subtract_fusion.1 = (f32[4,256,32,128]{1,3,2,0:T(8,128)S(1)}, f32[4,256,32,128]{1,3,2,0:T(8,128)}) fusion(f32[4,256,32,256]{1,3,2,0:T(8,128)} %fusion.8, f32[32,128]{1,0:T(8,128)S(1)} %get-tuple-element.37, f32[32,128]{1,0:T(8,128)S(1)} %get-tuple-element.38), kind=kLoop, calls=%fused_computation.18 | loop fusion | flops 25165824 | bytes 67141632 | tf_op jit(solution)/shard_map/sub | solution.py:40
  140.0 18.5 %pad_maximum_fusion = f32[4,256,64,128]{1,3,2,0:T(8,128)} fusion(f32[4,256,32,128]{1,3,2,0:T(8,128)} %get-tuple-element.14, f32[4,256,32,128]{1,3,2,0:T(8,128)S(1)} %get-tuple-element.13), kind=kLoop, calls=%fused_computation | loop fusion | flops 8388608 | bytes 67108864 | tf_op jit(solution)/shard_map/concatenate | solution.py:42
  158.5 31.8 %copy.178 = f32[4,256,64,128]{3,2,1,0:T(8,128)} copy(f32[4,256,64,128]{1,3,2,0:T(8,128)} %pad_maximum_fusion) | data formatting | bytes 67108864 | tf_op jit(solution)/shard_map/concatenate | solution.py:42
  190.3 24.1 %convolution_bitcast_fusion = f32[4,256,32,128]{3,2,1,0:T(8,128)S(1)} fusion(f32[4,256,64,128]{3,2,1,0:T(8,128)} %copy.178, f32[32,16]{0,1:T(8,128)S(1)} %get-tuple-element.40, f32[32,16]{0,1:T(8,128)S(1)} %get-tuple-element.39, f32[32,16]{0,1:T(8,128)S(1)} %fusion.98), kind=kOutput, calls=%fused_computation.36 | convolution fusion | flops 3221231616 | bytes 50337792 | tf_op jit(solution)/shard_map/...pk,pj->...jk/dot_general | solution.py:21
  244.7 175.5 %all-to-all-done.1 = f32[4,256,2048]{1,0,2:T(4,128)} async-done(((f32[4,256,2048]{1,0,2:T(4,128)}), f32[4,256,2048]{1,0,2:T(4,128)}, u32[]{:S(2)}, u32[]{:S(2)}) %all-to-all-start.1) | async-done | bytes 8388640 | tf_op jit(solution)/shard_map/all_to_all | solution.py:81
  447.6 18.5 %all_to_all.165 = f32[4,2048,256]{1,0,2:T(4,128)} all-to-all(f32[4,2048,256]{1,0,2:T(4,128)} %copy.182), channel_id=1, replica_groups=mesh['tiles'=2,'row'=8,'col'=2] {'col'}, dimensions={2} | all-to-all | bytes 16777216 | tf_op jit(solution)/shard_map/all_to_all | solution.py:80
  471.2 23.0 %fusion.110 = (bf16[1,4,1,128,4096]{4,3,2,1,0:T(8,128)(2,1)}, bf16[1,4,1,128,4096]{4,3,2,1,0:T(8,128)(2,1)}, bf16[1,4,1,128,4096]{4,3,2,1,0:T(8,128)(2,1)}, bf16...) fusion(bf16[2,4,4,128,4096]{4,3,2,1,0:T(8,128)(2,1)} %param.3), kind=kLoop, calls=%fused_computation.172 | loop fusion | bytes 67108864 | tf_op jit(solution)/shard_map/slice | solution.py:102
  571.8 19.7 %fusion.43 = f32[4,128,32,256]{3,1,2,0:T(8,128)} fusion(f32[4,128,128,32]{1,3,2,0:T(8,128)S(1)} %bitcast.133, f32[128,128]{0,1:T(8,128)S(1)} %copy-done.1, f32[128,128]{0,1:T(8,128)S(1)} %copy-done.3), kind=kOutput, calls=%fused_computation.67 | convolution fusion | flops 6442483712 | bytes 25296896 | tf_op jit(solution)/shard_map/...qp,qk->...pk/dot_general | solution.py:17
  591.5 63.4 %all-to-all-done.3 = f32[4,256,2048]{1,0,2:T(4,128)} async-done(((f32[4,256,2048]{1,0,2:T(4,128)}), f32[4,256,2048]{1,0,2:T(4,128)}, u32[]{:S(2)}, u32[]{:S(2)}) %all-to-all-start.3) | async-done | bytes 8388640 | tf_op jit(solution)/shard_map/all_to_all | solution.py:88
  715.7 19.5 %fusion.41 = f32[4,128,32,256]{3,1,2,0:T(8,128)} fusion(f32[4,128,128,32]{1,3,2,0:T(8,128)S(1)} %bitcast.132, f32[128,128]{0,1:T(8,128)S(1)} %copy-done.1, f32[128,128]{0,1:T(8,128)S(1)} %copy-done.3), kind=kOutput, calls=%fused_computation.65 | convolution fusion | flops 6442483712 | bytes 25296896 | tf_op jit(solution)/shard_map/...qp,qk->...pk/dot_general | solution.py:17
  735.2 19.1 %multiply_subtract_fusion.3 = (f32[4,128,32,128]{3,1,2,0:T(8,128)}, f32[4,128,32,128]{3,1,2,0:T(8,128)}) fusion(f32[32,128]{1,0:T(8,128)S(1)} %copy-done.11, f32[32,128]{1,0:T(8,128)S(1)} %copy-done.13, f32[4,128,32,256]{3,1,2,0:T(8,128)} %fusion.41, f32[4,128,32,256]{3,1,2,0:T(8,128)} %fusion.43), kind=kLoop, calls=%fused_computation.72 | loop fusion | flops 16777216 | bytes 50364416 | tf_op jit(solution)/shard_map/sub | solution.py:40
  766.2 33.5 %fusion.11 = f32[4,128,64,128]{3,2,1,0:T(8,128)} fusion(f32[4,128,64,128]{3,1,2,0:T(8,128)} %pad_maximum_fusion.2, f32[32,32]{0,1:T(8,128)S(1)} %get-tuple-element.42, f32[32,32]{0,1:T(8,128)S(1)} %get-tuple-element.41, f32[32,32]{0,1:T(8,128)S(1)} %fusion.95), kind=kOutput, calls=%fused_computation.37 | convolution fusion | flops 3221237760 | bytes 33566720 | tf_op jit(solution)/shard_map/...pk,pj->...jk/dot_general | solution.py:21
  834.9 17.6 %fusion.22 = (f32[4,128,128,32]{1,3,2,0:T(8,128)S(1)}, f32[4,128,128,32]{1,3,2,0:T(8,128)S(1)}) fusion(bf16[4,128,128,32]{1,3,2,0:T(8,128)(2,1)} %bitcast.169, bf16[4,128,128,32]{1,3,2,0:T(8,128)(2,1)} %bitcast.168, bf16[4,128,128,32]{1,3,2,0:T(8,128)(2,1)} %bitcast.167, bf16[4,128,128,32]{1,3,2,0:T(8,128)(2,1)} %bitcast.166, ...), kind=kLoop, calls=%fused_computation.42 | loop fusion | flops 79691776 | bytes 67108864 | tf_op jit(solution)/shard_map/add | solution.py:111
  852.5 19.4 %fusion.39 = f32[4,128,32,256]{3,1,2,0:T(8,128)} fusion(f32[4,128,128,32]{1,3,2,0:T(8,128)S(1)} %get-tuple-element.7, f32[128,128]{0,1:T(8,128)S(1)} %get-tuple-element.43, f32[128,128]{0,1:T(8,128)S(1)} %get-tuple-element.44), kind=kOutput, calls=%fused_computation.63 | convolution fusion | flops 6442483712 | bytes 25296896 | tf_op jit(solution)/shard_map/...qp,qk->...pk/dot_general | solution.py:17
  872.0 19.5 %fusion.37 = f32[4,128,32,256]{3,1,2,0:T(8,128)} fusion(f32[4,128,128,32]{1,3,2,0:T(8,128)S(1)} %get-tuple-element.8, f32[128,128]{0,1:T(8,128)S(1)} %get-tuple-element.43, f32[128,128]{0,1:T(8,128)S(1)} %get-tuple-element.44), kind=kOutput, calls=%fused_computation.61 | convolution fusion | flops 6442483712 | bytes 25296896 | tf_op jit(solution)/shard_map/...qp,qk->...pk/dot_general | solution.py:17
  891.5 19.1 %multiply_subtract_fusion.2 = (f32[4,128,32,128]{3,1,2,0:T(8,128)}, f32[4,128,32,128]{3,1,2,0:T(8,128)}) fusion(f32[32,128]{1,0:T(8,128)S(1)} %copy-done.8, f32[32,128]{1,0:T(8,128)S(1)} %copy-done.9, f32[4,128,32,256]{3,1,2,0:T(8,128)} %fusion.37, f32[4,128,32,256]{3,1,2,0:T(8,128)} %fusion.39), kind=kLoop, calls=%fused_computation.70 | loop fusion | flops 16777216 | bytes 50364416 | tf_op jit(solution)/shard_map/sub | solution.py:40
  922.5 33.5 %fusion.14 = f32[4,128,64,128]{3,2,1,0:T(8,128)} fusion(f32[4,128,64,128]{3,1,2,0:T(8,128)} %pad_maximum_fusion.3, f32[32,32]{0,1:T(8,128)S(1)} %copy-done.6, f32[32,32]{0,1:T(8,128)S(1)} %copy-done.14, f32[32,32]{0,1:T(8,128)S(1)} %copy-done.4), kind=kOutput, calls=%fused_computation.38 | convolution fusion | flops 3221237760 | bytes 33566720 | tf_op jit(solution)/shard_map/...pk,pj->...jk/dot_general | solution.py:21
  987.9 175.7 %all-to-all-done.5 = f32[4,128,4096]{1,0,2:T(4,128)} async-done(((f32[4,128,4096]{1,0,2:T(4,128)}), f32[4,128,4096]{1,0,2:T(4,128)}, u32[]{:S(2)}, u32[]{:S(2)}) %all-to-all-start.5) | async-done | bytes 8388640 | tf_op jit(solution)/shard_map/all_to_all | solution.py:117
  1189.9 18.5 %all_to_all.167 = f32[4,1024,512]{1,0,2:T(4,128)} all-to-all(f32[4,1024,512]{1,0,2:T(4,128)} %copy.221), channel_id=1, replica_groups=mesh['tiles'=2,'row'=8,'col'=2] {'col'}, dimensions={2} | all-to-all | bytes 16777216 | tf_op jit(solution)/shard_map/all_to_all | solution.py:116
  1241.4 155.6 %all-to-all-done.7 = f32[4,128,4096]{1,0,2:T(4,128)} async-done(((f32[4,128,4096]{1,0,2:T(4,128)}), f32[4,128,4096]{1,0,2:T(4,128)}, u32[]{:S(2)}, u32[]{:S(2)}) %all-to-all-start.7) | async-done | bytes 8388640 | tf_op jit(solution)/shard_map/all_to_all | solution.py:124
  1456.7 31.3 %fusion.33 = f32[4,256,32,256]{3,1,2,0:T(8,128)} fusion(f32[4,256,64,32]{1,3,2,0:T(8,128)S(1)} %bitcast.141, f32[64,128]{1,0:T(8,128)S(1)} %get-tuple-element.49, f32[64,128]{1,0:T(8,128)S(1)} %get-tuple-element.50), kind=kOutput, calls=%fused_computation.57 | convolution fusion | flops 6442467328 | bytes 42008576 | tf_op jit(solution)/shard_map/...qp,qk->...pk/dot_general | solution.py:17
  1488.1 31.5 %fusion.35 = f32[4,256,32,256]{3,1,2,0:T(8,128)} fusion(f32[4,256,64,32]{1,3,2,0:T(8,128)S(1)} %bitcast.140, f32[64,128]{1,0:T(8,128)S(1)} %get-tuple-element.49, f32[64,128]{1,0:T(8,128)S(1)} %get-tuple-element.50), kind=kOutput, calls=%fused_computation.59 | convolution fusion | flops 6442467328 | bytes 42008576 | tf_op jit(solution)/shard_map/...qp,qk->...pk/dot_general | solution.py:17
  1519.6 34.7 %multiply_subtract_fusion = (f32[4,256,32,128]{3,1,2,0:T(8,128)}, f32[4,256,32,128]{3,1,2,0:T(8,128)}) fusion(f32[32,128]{1,0:T(8,128)S(1)} %copy-done.8, f32[32,128]{1,0:T(8,128)S(1)} %copy-done.9, f32[4,256,32,256]{3,1,2,0:T(8,128)} %fusion.33, f32[4,256,32,256]{3,1,2,0:T(8,128)} %fusion.35), kind=kLoop, calls=%fused_computation.16 | loop fusion | flops 33554432 | bytes 100696064 | tf_op jit(solution)/shard_map/sub | solution.py:40
  1554.3 23.3 %pad_maximum_fusion.1 = f32[4,256,64,128]{3,1,2,0:T(8,128)} fusion(f32[4,256,32,128]{3,1,2,0:T(8,128)} %get-tuple-element.6, f32[4,256,32,128]{3,1,2,0:T(8,128)} %get-tuple-element.5), kind=kLoop, calls=%fused_computation.1 | loop fusion | flops 8388608 | bytes 67108864 | tf_op jit(solution)/shard_map/concatenate | solution.py:42
  1577.6 47.1 %multiply_bitcast_fusion = f32[4,256,32,128]{3,2,1,0:T(8,128)} fusion(f32[4,256,64,128]{3,1,2,0:T(8,128)} %pad_maximum_fusion.1, f32[32,32]{0,1:T(8,128)S(1)} %copy-done.5, f32[32,32]{0,1:T(8,128)S(1)} %copy-done.7), kind=kOutput, calls=%fused_computation.14 | convolution fusion | flops 3225421824 | bytes 50339840 | tf_op jit(solution)/shard_map/...pk,pj->...jk/dot_general | solution.py:21
  1624.7 15.5 copy.255
  1640.2 31.6 %all_to_all.169 = f32[4,256,4096]{1,0,2:T(4,128)} all-to-all(f32[4,256,4096]{1,0,2:T(4,128)} %bitcast.136), channel_id=1, replica_groups=mesh['tiles'=2,'row'=8,'col'=2] {'col'}, dimensions={2} | all-to-all | bytes 33554432 | tf_op jit(solution)/shard_map/all_to_all | solution.py:135
  1671.8 19.2 %copy.236 = f32[4,2,256,2048]{3,2,1,0:T(8,128)} copy(f32[4,2,256,2048]{2,0,3,1:T(4,128)} %bitcast.137) | data formatting | bytes 33554432 | tf_op jit(solution)/shard_map/all_to_all | solution.py:135
  (103 shorter events, 434.2 us)
Async XLA Ops:
  20.9 23.2 %all-to-all-start = ((f32[4,512,2048]{2,0,1:T(4,128)}), f32[4,512,2048]{2,0,1:T(4,128)}, u32[]{:S(2)}, u32[]{:S(2)}) async-start(f32[4,512,2048]{2,0,1:T(4,128)} %copy.174), calls=%async_computation | async-start | bytes 33554432 | tf_op jit(solution)/shard_map/all_to_all | solution.py:71
  30.9 91.5 %copy-start.10 = (f32[32,128]{1,0:T(8,128)}, f32[32,128]{1,0:T(8,128)S(1)}, u32[]{:S(2)}) copy-start(f32[32,128]{1,0:T(8,128)S(1)} %get-tuple-element.37) | copy-start | bytes 49156
  30.9 91.5 %copy-start.12 = (f32[32,128]{1,0:T(8,128)}, f32[32,128]{1,0:T(8,128)S(1)}, u32[]{:S(2)}) copy-start(f32[32,128]{1,0:T(8,128)S(1)} %get-tuple-element.38) | copy-start | bytes 49156
  31.2 47.1 %copy-start = (f32[128,128]{0,1:T(8,128)}, f32[128,128]{0,1:T(8,128)S(1)}, u32[]{:S(2)}) copy-start(f32[128,128]{0,1:T(8,128)S(1)} %get-tuple-element.35) | copy-start | bytes 196612
  31.2 47.1 %copy-start.2 = (f32[128,128]{0,1:T(8,128)}, f32[128,128]{0,1:T(8,128)S(1)}, u32[]{:S(2)}) copy-start(f32[128,128]{0,1:T(8,128)S(1)} %get-tuple-element.36) | copy-start | bytes 196612
  229.5 190.7 %all-to-all-start.1 = ((f32[4,256,2048]{1,0,2:T(4,128)}), f32[4,256,2048]{1,0,2:T(4,128)}, u32[]{:S(2)}, u32[]{:S(2)}) async-start(f32[4,256,2048]{1,0,2:T(4,128)} %bitcast.144), calls=%async_computation.1 | async-start | bytes 16777216 | tf_op jit(solution)/shard_map/all_to_all | solution.py:81
  466.1 188.8 %all-to-all-start.3 = ((f32[4,256,2048]{1,0,2:T(4,128)}), f32[4,256,2048]{1,0,2:T(4,128)}, u32[]{:S(2)}, u32[]{:S(2)}) async-start(f32[4,256,2048]{1,0,2:T(4,128)} %bitcast.142), calls=%async_computation.3 | async-start | bytes 16777216 | tf_op jit(solution)/shard_map/all_to_all | solution.py:88
  567.8 4.0 copy-start.1
  567.8 4.0 copy-start.3
  715.7 19.6 %copy-start.11 = (f32[32,128]{1,0:T(8,128)S(1)}, f32[32,128]{1,0:T(8,128)}, u32[]{:S(2)}) copy-start(f32[32,128]{1,0:T(8,128)} %copy-done.10) | copy-start | bytes 49156
  715.7 19.6 %copy-start.13 = (f32[32,128]{1,0:T(8,128)S(1)}, f32[32,128]{1,0:T(8,128)}, u32[]{:S(2)}) copy-start(f32[32,128]{1,0:T(8,128)} %copy-done.12) | copy-start | bytes 49156
  871.9 19.5 %copy-start.8 = (f32[32,128]{1,0:T(8,128)S(1)}, f32[32,128]{1,0:T(8,128)}, u32[]{:S(2)}) copy-start(f32[32,128]{1,0:T(8,128)} %get-tuple-element.45) | copy-start | bytes 49156
  872.0 19.5 %copy-start.9 = (f32[32,128]{1,0:T(8,128)S(1)}, f32[32,128]{1,0:T(8,128)}, u32[]{:S(2)}) copy-start(f32[32,128]{1,0:T(8,128)} %get-tuple-element.46) | copy-start | bytes 49156
  910.6 11.9 copy-start.4
  910.6 11.9 copy-start.6
  910.6 11.9 copy-start.14
  975.0 188.6 %all-to-all-start.5 = ((f32[4,128,4096]{1,0,2:T(4,128)}), f32[4,128,4096]{1,0,2:T(4,128)}, u32[]{:S(2)}, u32[]{:S(2)}) async-start(f32[4,128,4096]{1,0,2:T(4,128)} %bitcast.145), calls=%async_computation.5 | async-start | bytes 16777216 | tf_op jit(solution)/shard_map/all_to_all | solution.py:117
  1208.4 188.6 %all-to-all-start.7 = ((f32[4,128,4096]{1,0,2:T(4,128)}), f32[4,128,4096]{1,0,2:T(4,128)}, u32[]{:S(2)}, u32[]{:S(2)}) async-start(f32[4,128,4096]{1,0,2:T(4,128)} %bitcast.143), calls=%async_computation.7 | async-start | bytes 16777216 | tf_op jit(solution)/shard_map/all_to_all | solution.py:124
  1452.6 35.5 %slice-start = ((s8[8388608]{0:T(1024)(128)(4,1)}), s8[4194304]{0:T(1024)(128)(4,1)S(1)}, s32[]{:S(2)}) async-start(s8[8388608]{0:T(1024)(128)(4,1)} %bitcast.138), calls=%async_computation.10 | async-start | bytes 8388608
  1456.7 31.3 %slice-start.1 = ((s8[8388608]{0:T(1024)(128)(4,1)}), s8[4194304]{0:T(1024)(128)(4,1)S(1)}, s32[]{:S(2)}) async-start(s8[8388608]{0:T(1024)(128)(4,1)} %bitcast.138), calls=%async_computation.11 | async-start | bytes 8388608
  1554.3 23.3 %copy-start.5 = (f32[32,32]{0,1:T(8,128)S(1)}, f32[32,32]{0,1:T(8,128)}, u32[]{:S(2)}) copy-start(f32[32,32]{0,1:T(8,128)} %fusion.94) | copy-start | bytes 12292
  1554.3 23.3 %copy-start.7 = (f32[32,32]{0,1:T(8,128)S(1)}, f32[32,32]{0,1:T(8,128)}, u32[]{:S(2)}) copy-start(f32[32,32]{0,1:T(8,128)} %get-tuple-element.48) | copy-start | bytes 12292
where the time goes:
time: 1700 us; the launch traced here: 1690 us
  waiting for transfers between devices  583 us (34%)
  local copies, waits for them, and re-layouts  482 us (28%)
  matrix products  323 us (19%)
  other arithmetic  177 us (10%)
  blocking collectives  93.3 us (5%)
  starting transfers between devices  32.1 us (2%)
    dot_general x7, matrix products, contract_first(): jnp.einsum('...qp,qk->...pk', values, table, precision=lax.Precision.HIGH...  185 us
    all_to_all x1, waiting for transfers between devices, shards(): lax.all_to_all(back_real, 'row', split_axis=2, concat_axis=1, tiled=True)  176 us
    all_to_all x1, waiting for transfers between devices, shards(): lax.all_to_all(spec_real, 'row', split_axis=2, concat_axis=1, tiled=True)  175 us
    all_to_all x1, waiting for transfers between devices, shards(): lax.all_to_all(back_imag, 'row', split_axis=2, concat_axis=1, tiled=True)  156 us
    dot_general x4, matrix products, contract_second(): jnp.einsum('...pk,pj->...jk', values, table, precision=lax.Precision.HIGH...  138 us
    sub x4, other arithmetic, fourier(): turned_real = part_real * twist_cos - part_imag * twist_sin  90.5 us
    unnamed x43, local copies, waits for them, and re-layouts  71.9 us
    concatenate x4, other arithmetic, fourier(): stacked = jnp.concatenate([turned_real, turned_imag], axis=-2)  65.5 us
  transfers between devices with their start and end apart: 5, of which 5 were waited for; matrix products, arithmetic and copies ran while one was open for 10% of the time, Pallas kernels for 0%

commit v1 on v0

--- a/solution.py
+++ b/solution.py
@@ -3,6 +3,10 @@
 import jax.numpy as jnp
 from jax import lax
 from jax.sharding import PartitionSpec as P
+
+derive_terms = lambda target: jnp.concatenate(
+    lax.all_to_all(jnp.stack(jnp.split(target, lax.psum(1, "col"), 2), 0), "col", 0, 0), 1
+)
 
 
 def phase_pair(first_len, second_len, period, sign):
@@ -84,13 +88,7 @@
             concat_axis=1,
             tiled=True,
         ),
-        lax.all_to_all(
-            lax.all_to_all(spec_imag, "row", split_axis=2, concat_axis=1, tiled=True),
-            "col",
-            split_axis=2,
-            concat_axis=1,
-            tiled=True,
-        ),
+        derive_terms(lax.all_to_all(spec_imag, "row", split_axis=2, concat_axis=1, tiled=True)),
     )
     line_real = reorder_blocks(moved_real, row_count, col_count)
     line_imag = reorder_blocks(moved_imag, row_count, col_count)

time: 1700 us -> 1680 us (0.988)
  local copies, waits for them, and re-layouts: 482 us -> 456 us
where the time goes in v1:
time: 1680 us; the launch traced here: 1660 us
  waiting for transfers between devices  583 us (35%)
  local copies, waits for them, and re-layouts  456 us (27%)
  matrix products  323 us (19%)
  other arithmetic  178 us (11%)
  blocking collectives  91.7 us (5%)
  starting transfers between devices  32.1 us (2%)
    dot_general x7, matrix products, contract_first(): jnp.einsum('...qp,qk->...pk', values, table, precision=lax.Precision.HIGH...  185 us
    all_to_all x1, waiting for transfers between devices, shards(): lax.all_to_all(back_real, 'row', split_axis=2, concat_axis=1, tiled=True)  176 us
    all_to_all x1, waiting for transfers between devices, shards(): lax.all_to_all(spec_real, 'row', split_axis=2, concat_axis=1, tiled=True)  175 us
    all_to_all x1, waiting for transfers between devices, shards(): lax.all_to_all(back_imag, 'row', split_axis=2, concat_axis=1, tiled=True)  156 us
    dot_general x4, matrix products, contract_second(): jnp.einsum('...pk,pj->...jk', values, table, precision=lax.Precision.HIGH...  138 us
    sub x4, other arithmetic, fourier(): turned_real = part_real * twist_cos - part_imag * twist_sin  90.6 us
    unnamed x43, local copies, waits for them, and re-layouts  71.9 us
    concatenate x4, other arithmetic, fourier(): stacked = jnp.concatenate([turned_real, turned_imag], axis=-2)  65.7 us
  transfers between devices with their start and end apart: 5, of which 5 were waited for; matrix products, arithmetic and copies ran while one was open for 10% of the time, Pallas kernels for 0%

profile of v1, /device:TPU:0, one launch (start us, length us, event | category | flops | bytes accessed | tf_op | source)
XLA Modules:
  0.0 1664.7 jit_solution(13805459004806867108)
XLA Ops:
  0.0 20.9 %copy.173 = f32[4,512,2048]{2,0,1:T(4,128)} copy(f32[4,512,2048]{2,1,0:T(8,128)} %param.2) | data formatting | bytes 33554432 | tf_op args[0]
  44.1 17.8 %copy.174 = f32[4,512,2048]{2,1,0:T(8,128)} copy(f32[4,512,2048]{2,0,1:T(4,128)} %all-to-all-done) | data formatting | bytes 33554432 | tf_op jit(solution)/shard_map/all_to_all | solution.py:75
  61.9 16.4 copy.175
  78.3 44.1 %fusion.8 = f32[4,256,32,256]{1,3,2,0:T(8,128)} fusion(f32[4,256,128,32]{1,3,2,0:T(8,128)} %bitcast.137, f32[128,128]{0,1:T(8,128)S(1)} %get-tuple-element.37, f32[128,128]{0,1:T(8,128)S(1)} %get-tuple-element.38), kind=kOutput, calls=%fused_computation.19 | convolution fusion | flops 12884934656 | bytes 50462720 | tf_op jit(solution)/shard_map/...qp,qk->...pk/dot_general | solution.py:21
  122.4 17.6 %multiply_subtract_fusion.1 = (f32[4,256,32,128]{1,3,2,0:T(8,128)S(1)}, f32[4,256,32,128]{1,3,2,0:T(8,128)}) fusion(f32[4,256,32,256]{1,3,2,0:T(8,128)} %fusion.8, f32[32,128]{1,0:T(8,128)S(1)} %get-tuple-element.39, f32[32,128]{1,0:T(8,128)S(1)} %get-tuple-element.40), kind=kLoop, calls=%fused_computation.18 | loop fusion | flops 25165824 | bytes 67141632 | tf_op jit(solution)/shard_map/sub | solution.py:44
  140.0 18.6 %pad_maximum_fusion = f32[4,256,64,128]{1,3,2,0:T(8,128)} fusion(f32[4,256,32,128]{1,3,2,0:T(8,128)} %get-tuple-element.14, f32[4,256,32,128]{1,3,2,0:T(8,128)S(1)} %get-tuple-element.13), kind=kLoop, calls=%fused_computation | loop fusion | flops 8388608 | bytes 67108864 | tf_op jit(solution)/shard_map/concatenate | solution.py:46
  158.6 31.9 %copy.177 = f32[4,256,64,128]{3,2,1,0:T(8,128)} copy(f32[4,256,64,128]{1,3,2,0:T(8,128)} %pad_maximum_fusion) | data formatting | bytes 67108864 | tf_op jit(solution)/shard_map/concatenate | solution.py:46
  190.5 24.1 %convolution_bitcast_fusion = f32[4,256,32,128]{3,2,1,0:T(8,128)S(1)} fusion(f32[4,256,64,128]{3,2,1,0:T(8,128)} %copy.177, f32[32,16]{0,1:T(8,128)S(1)} %get-tuple-element.42, f32[32,16]{0,1:T(8,128)S(1)} %get-tuple-element.41, f32[32,16]{0,1:T(8,128)S(1)} %fusion.98), kind=kOutput, calls=%fused_computation.36 | convolution fusion | flops 3221231616 | bytes 50337792 | tf_op jit(solution)/shard_map/...pk,pj->...jk/dot_general | solution.py:25
  244.9 175.5 %all-to-all-done.1 = f32[4,256,2048]{1,0,2:T(4,128)} async-done(((f32[4,256,2048]{1,0,2:T(4,128)}), f32[4,256,2048]{1,0,2:T(4,128)}, u32[]{:S(2)}, u32[]{:S(2)}) %all-to-all-start.1) | async-done | bytes 8388640 | tf_op jit(solution)/shard_map/all_to_all | solution.py:85
  447.7 18.5 %all_to_all.155 = f32[4,2048,256]{1,0,2:T(4,128)} all-to-all(f32[4,2048,256]{1,0,2:T(4,128)} %copy.181), channel_id=1, replica_groups=mesh['tiles'=2,'row'=8,'col'=2] {'col'}, dimensions={2} | all-to-all | bytes 16777216 | tf_op jit(solution)/shard_map/all_to_all | solution.py:84
  471.4 23.0 %fusion.110 = (bf16[1,4,1,128,4096]{4,3,2,1,0:T(8,128)(2,1)}, bf16[1,4,1,128,4096]{4,3,2,1,0:T(8,128)(2,1)}, bf16[1,4,1,128,4096]{4,3,2,1,0:T(8,128)(2,1)}, bf16...) fusion(bf16[2,4,4,128,4096]{4,3,2,1,0:T(8,128)(2,1)} %param.3), kind=kLoop, calls=%fused_computation.175 | loop fusion | bytes 67108864 | tf_op jit(solution)/shard_map/slice | solution.py:100
  572.0 19.7 %fusion.43 = f32[4,128,32,256]{3,1,2,0:T(8,128)} fusion(f32[4,128,128,32]{1,3,2,0:T(8,128)S(1)} %bitcast.136, f32[128,128]{0,1:T(8,128)S(1)} %copy-done.1, f32[128,128]{0,1:T(8,128)S(1)} %copy-done.3), kind=kOutput, calls=%fused_computation.68 | convolution fusion | flops 6442483712 | bytes 25296896 | tf_op jit(solution)/shard_map/...qp,qk->...pk/dot_general | solution.py:21
  591.6 63.4 %all-to-all-done.3 = f32[4,256,2048]{1,0,2:T(4,128)} async-done(((f32[4,256,2048]{1,0,2:T(4,128)}), f32[4,256,2048]{1,0,2:T(4,128)}, u32[]{:S(2)}, u32[]{:S(2)}) %all-to-all-start.3) | async-done | bytes 8388640 | tf_op jit(solution)/shard_map/all_to_all | solution.py:91
  688.6 19.5 %fusion.41 = f32[4,128,32,256]{3,1,2,0:T(8,128)} fusion(f32[4,128,128,32]{1,3,2,0:T(8,128)S(1)} %bitcast.135, f32[128,128]{0,1:T(8,128)S(1)} %copy-done.1, f32[128,128]{0,1:T(8,128)S(1)} %copy-done.3), kind=kOutput, calls=%fused_computation.66 | convolution fusion | flops 6442483712 | bytes 25296896 | tf_op jit(solution)/shard_map/...qp,qk->...pk/dot_general | solution.py:21
  708.2 19.1 %multiply_subtract_fusion.3 = (f32[4,128,32,128]{3,1,2,0:T(8,128)}, f32[4,128,32,128]{3,1,2,0:T(8,128)}) fusion(f32[32,128]{1,0:T(8,128)S(1)} %copy-done.11, f32[32,128]{1,0:T(8,128)S(1)} %copy-done.13, f32[4,128,32,256]{3,1,2,0:T(8,128)} %fusion.41, f32[4,128,32,256]{3,1,2,0:T(8,128)} %fusion.43), kind=kLoop, calls=%fused_computation.73 | loop fusion | flops 16777216 | bytes 50364416 | tf_op jit(solution)/shard_map/sub | solution.py:44
  739.1 33.5 %fusion.11 = f32[4,128,64,128]{3,2,1,0:T(8,128)} fusion(f32[4,128,64,128]{3,1,2,0:T(8,128)} %pad_maximum_fusion.2, f32[32,32]{0,1:T(8,128)S(1)} %get-tuple-element.44, f32[32,32]{0,1:T(8,128)S(1)} %get-tuple-element.43, f32[32,32]{0,1:T(8,128)S(1)} %fusion.95), kind=kOutput, calls=%fused_computation.37 | convolution fusion | flops 3221237760 | bytes 33566720 | tf_op jit(solution)/shard_map/...pk,pj->...jk/dot_general | solution.py:25
  807.8 17.6 %fusion.22 = (f32[4,128,128,32]{1,3,2,0:T(8,128)S(1)}, f32[4,128,128,32]{1,3,2,0:T(8,128)S(1)}) fusion(bf16[4,128,128,32]{1,3,2,0:T(8,128)(2,1)} %bitcast.171, bf16[4,128,128,32]{1,3,2,0:T(8,128)(2,1)} %bitcast.170, bf16[4,128,128,32]{1,3,2,0:T(8,128)(2,1)} %bitcast.169, bf16[4,128,128,32]{1,3,2,0:T(8,128)(2,1)} %bitcast.168, ...), kind=kLoop, calls=%fused_computation.42 | loop fusion | flops 79691776 | bytes 67108864 | tf_op jit(solution)/shard_map/add | solution.py:109
  825.4 19.4 %fusion.39 = f32[4,128,32,256]{3,1,2,0:T(8,128)} fusion(f32[4,128,128,32]{1,3,2,0:T(8,128)S(1)} %get-tuple-element.7, f32[128,128]{0,1:T(8,128)S(1)} %get-tuple-element.45, f32[128,128]{0,1:T(8,128)S(1)} %get-tuple-element.46), kind=kOutput, calls=%fused_computation.64 | convolution fusion | flops 6442483712 | bytes 25296896 | tf_op jit(solution)/shard_map/...qp,qk->...pk/dot_general | solution.py:21
  844.9 19.5 %fusion.37 = f32[4,128,32,256]{3,1,2,0:T(8,128)} fusion(f32[4,128,128,32]{1,3,2,0:T(8,128)S(1)} %get-tuple-element.8, f32[128,128]{0,1:T(8,128)S(1)} %get-tuple-element.45, f32[128,128]{0,1:T(8,128)S(1)} %get-tuple-element.46), kind=kOutput, calls=%fused_computation.62 | convolution fusion | flops 6442483712 | bytes 25296896 | tf_op jit(solution)/shard_map/...qp,qk->...pk/dot_general | solution.py:21
  864.4 19.1 %multiply_subtract_fusion.2 = (f32[4,128,32,128]{3,1,2,0:T(8,128)}, f32[4,128,32,128]{3,1,2,0:T(8,128)}) fusion(f32[32,128]{1,0:T(8,128)S(1)} %copy-done.8, f32[32,128]{1,0:T(8,128)S(1)} %copy-done.9, f32[4,128,32,256]{3,1,2,0:T(8,128)} %fusion.37, f32[4,128,32,256]{3,1,2,0:T(8,128)} %fusion.39), kind=kLoop, calls=%fused_computation.71 | loop fusion | flops 16777216 | bytes 50364416 | tf_op jit(solution)/shard_map/sub | solution.py:44
  895.4 33.5 %fusion.14 = f32[4,128,64,128]{3,2,1,0:T(8,128)} fusion(f32[4,128,64,128]{3,1,2,0:T(8,128)} %pad_maximum_fusion.3, f32[32,32]{0,1:T(8,128)S(1)} %copy-done.6, f32[32,32]{0,1:T(8,128)S(1)} %copy-done.14, f32[32,32]{0,1:T(8,128)S(1)} %copy-done.4), kind=kOutput, calls=%fused_computation.38 | convolution fusion | flops 3221237760 | bytes 33566720 | tf_op jit(solution)/shard_map/...pk,pj->...jk/dot_general | solution.py:25
  960.9 175.7 %all-to-all-done.5 = f32[4,128,4096]{1,0,2:T(4,128)} async-done(((f32[4,128,4096]{1,0,2:T(4,128)}), f32[4,128,4096]{1,0,2:T(4,128)}, u32[]{:S(2)}, u32[]{:S(2)}) %all-to-all-start.5) | async-done | bytes 8388640 | tf_op jit(solution)/shard_map/all_to_all | solution.py:115
  1162.9 18.5 %all_to_all.157 = f32[4,1024,512]{1,0,2:T(4,128)} all-to-all(f32[4,1024,512]{1,0,2:T(4,128)} %copy.217), channel_id=1, replica_groups=mesh['tiles'=2,'row'=8,'col'=2] {'col'}, dimensions={2} | all-to-all | bytes 16777216 | tf_op jit(solution)/shard_map/all_to_all | solution.py:114
  1214.3 155.6 %all-to-all-done.7 = f32[4,128,4096]{1,0,2:T(4,128)} async-done(((f32[4,128,4096]{1,0,2:T(4,128)}), f32[4,128,4096]{1,0,2:T(4,128)}, u32[]{:S(2)}, u32[]{:S(2)}) %all-to-all-start.7) | async-done | bytes 8388640 | tf_op jit(solution)/shard_map/all_to_all | solution.py:122
  1429.7 31.4 %fusion.33 = f32[4,256,32,256]{3,1,2,0:T(8,128)} fusion(f32[4,256,64,32]{1,3,2,0:T(8,128)S(1)} %bitcast.144, f32[64,128]{1,0:T(8,128)S(1)} %get-tuple-element.51, f32[64,128]{1,0:T(8,128)S(1)} %get-tuple-element.52), kind=kOutput, calls=%fused_computation.58 | convolution fusion | flops 6442467328 | bytes 42008576 | tf_op jit(solution)/shard_map/...qp,qk->...pk/dot_general | solution.py:21
  1461.1 31.6 %fusion.35 = f32[4,256,32,256]{3,1,2,0:T(8,128)} fusion(f32[4,256,64,32]{1,3,2,0:T(8,128)S(1)} %bitcast.143, f32[64,128]{1,0:T(8,128)S(1)} %get-tuple-element.51, f32[64,128]{1,0:T(8,128)S(1)} %get-tuple-element.52), kind=kOutput, calls=%fused_computation.60 | convolution fusion | flops 6442467328 | bytes 42008576 | tf_op jit(solution)/shard_map/...qp,qk->...pk/dot_general | solution.py:21
  1492.7 34.7 %multiply_subtract_fusion = (f32[4,256,32,128]{3,1,2,0:T(8,128)}, f32[4,256,32,128]{3,1,2,0:T(8,128)}) fusion(f32[32,128]{1,0:T(8,128)S(1)} %copy-done.8, f32[32,128]{1,0:T(8,128)S(1)} %copy-done.9, f32[4,256,32,256]{3,1,2,0:T(8,128)} %fusion.33, f32[4,256,32,256]{3,1,2,0:T(8,128)} %fusion.35), kind=kLoop, calls=%fused_computation.16 | loop fusion | flops 33554432 | bytes 100696064 | tf_op jit(solution)/shard_map/sub | solution.py:44
  1527.5 23.3 %pad_maximum_fusion.1 = f32[4,256,64,128]{3,1,2,0:T(8,128)} fusion(f32[4,256,32,128]{3,1,2,0:T(8,128)} %get-tuple-element.6, f32[4,256,32,128]{3,1,2,0:T(8,128)} %get-tuple-element.5), kind=kLoop, calls=%fused_computation.1 | loop fusion | flops 8388608 | bytes 67108864 | tf_op jit(solution)/shard_map/concatenate | solution.py:46
  1550.8 47.1 %multiply_bitcast_fusion = f32[4,256,32,128]{3,2,1,0:T(8,128)} fusion(f32[4,256,64,128]{3,1,2,0:T(8,128)} %pad_maximum_fusion.1, f32[32,32]{0,1:T(8,128)S(1)} %copy-done.5, f32[32,32]{0,1:T(8,128)S(1)} %copy-done.7), kind=kOutput, calls=%fused_computation.14 | convolution fusion | flops 3225421824 | bytes 50339840 | tf_op jit(solution)/shard_map/...pk,pj->...jk/dot_general | solution.py:25
  1597.9 15.5 copy.251
  1613.4 31.6 %all_to_all.159 = f32[4,256,4096]{1,0,2:T(4,128)} all-to-all(f32[4,256,4096]{1,0,2:T(4,128)} %bitcast.139), channel_id=1, replica_groups=mesh['tiles'=2,'row'=8,'col'=2] {'col'}, dimensions={2} | all-to-all | bytes 33554432 | tf_op jit(solution)/shard_map/all_to_all | solution.py:133
  1645.1 19.2 %copy.232 = f32[4,2,256,2048]{3,2,1,0:T(8,128)} copy(f32[4,2,256,2048]{2,0,3,1:T(4,128)} %bitcast.140) | data formatting | bytes 33554432 | tf_op jit(solution)/shard_map/all_to_all | solution.py:133
  (102 shorter events, 406.9 us)
Async XLA Ops:
  20.9 23.2 %all-to-all-start = ((f32[4,512,2048]{2,0,1:T(4,128)}), f32[4,512,2048]{2,0,1:T(4,128)}, u32[]{:S(2)}, u32[]{:S(2)}) async-start(f32[4,512,2048]{2,0,1:T(4,128)} %copy.173), calls=%async_computation | async-start | bytes 33554432 | tf_op jit(solution)/shard_map/all_to_all | solution.py:75
  30.9 91.5 %copy-start.10 = (f32[32,128]{1,0:T(8,128)}, f32[32,128]{1,0:T(8,128)S(1)}, u32[]{:S(2)}) copy-start(f32[32,128]{1,0:T(8,128)S(1)} %get-tuple-element.39) | copy-start | bytes 49156
  30.9 91.5 %copy-start.12 = (f32[32,128]{1,0:T(8,128)}, f32[32,128]{1,0:T(8,128)S(1)}, u32[]{:S(2)}) copy-start(f32[32,128]{1,0:T(8,128)S(1)} %get-tuple-element.40) | copy-start | bytes 49156
  31.2 47.1 %copy-start = (f32[128,128]{0,1:T(8,128)}, f32[128,128]{0,1:T(8,128)S(1)}, u32[]{:S(2)}) copy-start(f32[128,128]{0,1:T(8,128)S(1)} %get-tuple-element.37) | copy-start | bytes 196612
  31.2 47.1 %copy-start.2 = (f32[128,128]{0,1:T(8,128)}, f32[128,128]{0,1:T(8,128)S(1)}, u32[]{:S(2)}) copy-start(f32[128,128]{0,1:T(8,128)S(1)} %get-tuple-element.38) | copy-start | bytes 196612
  229.6 190.7 %all-to-all-start.1 = ((f32[4,256,2048]{1,0,2:T(4,128)}), f32[4,256,2048]{1,0,2:T(4,128)}, u32[]{:S(2)}, u32[]{:S(2)}) async-start(f32[4,256,2048]{1,0,2:T(4,128)} %bitcast.147), calls=%async_computation.1 | async-start | bytes 16777216 | tf_op jit(solution)/shard_map/all_to_all | solution.py:85
  466.2 188.8 %all-to-all-start.3 = ((f32[4,256,2048]{1,0,2:T(4,128)}), f32[4,256,2048]{1,0,2:T(4,128)}, u32[]{:S(2)}, u32[]{:S(2)}) async-start(f32[4,256,2048]{1,0,2:T(4,128)} %bitcast.145), calls=%async_computation.3 | async-start | bytes 16777216 | tf_op jit(solution)/shard_map/all_to_all | solution.py:91
  568.0 4.0 copy-start.1
  568.0 4.0 copy-start.3
  688.6 19.6 %copy-start.11 = (f32[32,128]{1,0:T(8,128)S(1)}, f32[32,128]{1,0:T(8,128)}, u32[]{:S(2)}) copy-start(f32[32,128]{1,0:T(8,128)} %copy-done.10) | copy-start | bytes 49156
  688.6 19.6 %copy-start.13 = (f32[32,128]{1,0:T(8,128)S(1)}, f32[32,128]{1,0:T(8,128)}, u32[]{:S(2)}) copy-start(f32[32,128]{1,0:T(8,128)} %copy-done.12) | copy-start | bytes 49156
  844.9 19.5 %copy-start.8 = (f32[32,128]{1,0:T(8,128)S(1)}, f32[32,128]{1,0:T(8,128)}, u32[]{:S(2)}) copy-start(f32[32,128]{1,0:T(8,128)} %get-tuple-element.47) | copy-start | bytes 49156
  844.9 19.5 %copy-start.9 = (f32[32,128]{1,0:T(8,128)S(1)}, f32[32,128]{1,0:T(8,128)}, u32[]{:S(2)}) copy-start(f32[32,128]{1,0:T(8,128)} %get-tuple-element.48) | copy-start | bytes 49156
  883.5 11.9 copy-start.4
  883.5 11.9 copy-start.6
  883.5 11.9 copy-start.14
  947.9 188.6 %all-to-all-start.5 = ((f32[4,128,4096]{1,0,2:T(4,128)}), f32[4,128,4096]{1,0,2:T(4,128)}, u32[]{:S(2)}, u32[]{:S(2)}) async-start(f32[4,128,4096]{1,0,2:T(4,128)} %bitcast.148), calls=%async_computation.5 | async-start | bytes 16777216 | tf_op jit(solution)/shard_map/all_to_all | solution.py:115
  1181.3 188.6 %all-to-all-start.7 = ((f32[4,128,4096]{1,0,2:T(4,128)}), f32[4,128,4096]{1,0,2:T(4,128)}, u32[]{:S(2)}, u32[]{:S(2)}) async-start(f32[4,128,4096]{1,0,2:T(4,128)} %bitcast.146), calls=%async_computation.7 | async-start | bytes 16777216 | tf_op jit(solution)/shard_map/all_to_all | solution.py:122
  1425.6 35.6 %slice-start = ((s8[8388608]{0:T(1024)(128)(4,1)}), s8[4194304]{0:T(1024)(128)(4,1)S(1)}, s32[]{:S(2)}) async-start(s8[8388608]{0:T(1024)(128)(4,1)} %bitcast.141), calls=%async_computation.10 | async-start | bytes 8388608
  1429.7 31.5 %slice-start.1 = ((s8[8388608]{0:T(1024)(128)(4,1)}), s8[4194304]{0:T(1024)(128)(4,1)S(1)}, s32[]{:S(2)}) async-start(s8[8388608]{0:T(1024)(128)(4,1)} %bitcast.141), calls=%async_computation.11 | async-start | bytes 8388608
  1527.5 23.3 %copy-start.5 = (f32[32,32]{0,1:T(8,128)S(1)}, f32[32,32]{0,1:T(8,128)}, u32[]{:S(2)}) copy-start(f32[32,32]{0,1:T(8,128)} %fusion.94) | copy-start | bytes 12292
  1527.5 23.3 %copy-start.7 = (f32[32,32]{0,1:T(8,128)S(1)}, f32[32,32]{0,1:T(8,128)}, u32[]{:S(2)}) copy-start(f32[32,32]{0,1:T(8,128)} %get-tuple-element.50) | copy-start | bytes 12292
